TPU v7x, 256 devices: a whole 4x4x8 slice. The times are simulated.
256 devices in a mesh: section: 2 (over z_hi), dp: 16 (over z_lo, y), tensor: 8 (over x, core).
Axes of the slice: x: 4, y: 4, z: 8 (z_hi: 2, z_lo: 4; z = z_hi * 4 + z_lo), core: 2. Of those that a mesh axis runs over, the one named last changes fastest.
Arguments:
- section_input: bfloat16 [2, 1024, 8192], P('section', 'tensor', 'dp'), may hold values from -40 to 40
- norm_gain_attn: bfloat16 [2, 8192], P('section', 'dp'), may hold values from 0.099609375 to 1.8984375
- w_query: bfloat16 [2, 8192, 4096], P('section', 'dp', 'tensor'), may hold values from -0.0625 to 0.0625
- key_value_weight: bfloat16 [2, 2, 8192, 512], P('section', None, 'dp'), may hold values from -0.0625 to 0.0625
- w_output: bfloat16 [2, 4096, 8192], P('section', 'tensor', 'dp'), may hold values from -0.09375 to 0.09375
- norm_gain_ffn: bfloat16 [2, 8192], P('section', 'dp'), may hold values from 0.099609375 to 1.8984375
- w_gate_up: bfloat16 [2, 2, 8192, 14336], P('section', None, 'dp', 'tensor'), may hold values from -0.0625 to 0.0625
- w_down: bfloat16 [2, 14336, 8192], P('section', 'tensor', 'dp'), may hold values from -0.046875 to 0.046875
Outputs:
- section_output: bfloat16 [2, 1024, 8192], P('section', 'tensor', 'dp')
All inputs are finite; a program needn't handle non-finite values.
Results may differ from a plain program's by a relative error of at most 0.019.
Values may be sent and summed in bfloat16 or wider, within the bound.
A program may use at most 64 MiB of HBM per device.

v0:
```python
import math
import jax
import jax.numpy as jnp
from jax import lax
from jax.sharding import PartitionSpec as P

HEAD_SIZE = 128
QUERY_HEADS = 32
KEY_VALUE_HEADS = 4
EPS = 1e-05
THETA = 500000.0


def from_behind(x, axis, by):
    count = lax.axis_size(axis)
    return lax.ppermute(x, axis, [(i, (i + by) % count) for i in range(count)])


def apply_rotary(value_states, token_positions):
    width = value_states.shape[-1]
    half = width // 2
    freqs = jnp.exp(-(2.0 * jnp.arange(half, dtype=jnp.float32) / width) * math.log(THETA))
    angles = token_positions.astype(jnp.float32)[:, None] * freqs[None, :]
    cosine = jnp.cos(angles)[:, None, :]
    sine = jnp.sin(angles)[:, None, :]
    first = value_states[..., :half]
    second = value_states[..., half:]
    return jnp.concatenate(
        [first * cosine - second * sine, second * cosine + first * sine], axis=-1
    )


def local(
    section_input,
    norm_gain_attn,
    w_query,
    key_value_weight,
    w_output,
    norm_gain_ffn,
    w_gate_up,
    w_down,
):
    tile = section_input[0]
    rows_dev = tile.shape[0]
    cols_dev = tile.shape[1]
    tensor_count = lax.axis_size("tensor")
    data_count = lax.axis_size("dp")
    seq_total = rows_dev * tensor_count
    query_rows = seq_total // data_count
    width_total = cols_dev * data_count
    head_dim = HEAD_SIZE
    heads_dev = w_query.shape[2] // head_dim
    group_heads = QUERY_HEADS // KEY_VALUE_HEADS
    kv_dev = max(1, heads_dev // group_heads)
    per_kv = heads_dev // kv_dev
    tensor_pos = lax.axis_index("tensor")
    data_pos = lax.axis_index("dp")
    kv_first = tensor_pos * heads_dev // group_heads
    key_cols = lax.dynamic_slice_in_dim(
        key_value_weight[0], kv_first * head_dim, kv_dev * head_dim, 2
    )
    w_columns = jnp.concatenate([w_query[0], key_cols[0], key_cols[1]], axis=1)
    gain_attn = norm_gain_attn[0].astype(jnp.float32)[None, :]
    gain_ffn = norm_gain_ffn[0].astype(jnp.float32)[None, :]
    query_cols = heads_dev * head_dim
    kv_cols = kv_dev * head_dim
    query_pos = data_pos * query_rows + jnp.arange(query_rows, dtype=jnp.int32)
    all_pos = jnp.arange(seq_total, dtype=jnp.int32)
    arrived = from_behind(tile, "section", 1)
    wide = arrived.astype(jnp.float32)
    squares = lax.psum(jnp.sum(wide * wide, axis=1), "dp")
    normed_input = (wide * lax.rsqrt(squares / width_total + EPS)[:, None] * gain_attn).astype(
        jnp.bfloat16
    )
    partial_qkv = jnp.dot(
        lax.all_gather(normed_input, "tensor", axis=0, tiled=True),
        w_columns,
        preferred_element_type=jnp.float32,
    )
    query_sum = lax.psum_scatter(
        partial_qkv[:, :query_cols].astype(jnp.bfloat16), "dp", scatter_dimension=0, tiled=True
    ).astype(jnp.float32)
    key_sum = lax.psum(partial_qkv[:, query_cols:].astype(jnp.bfloat16), "dp").astype(jnp.float32)
    keys = apply_rotary(key_sum[:, :kv_cols].reshape(seq_total, kv_dev, head_dim), all_pos).astype(
        jnp.bfloat16
    )
    value_states = key_sum[:, kv_cols:].reshape(seq_total, kv_dev, head_dim).astype(jnp.bfloat16)
    query_states = apply_rotary(
        query_sum.reshape(query_rows, heads_dev, head_dim), query_pos
    ).astype(jnp.bfloat16)
    grouped = query_states.reshape(query_rows, kv_dev, per_kv, head_dim)
    scores = jnp.einsum(
        "qkgd,skd->kgqs", grouped, keys, preferred_element_type=jnp.float32
    ) * head_dim ** (-0.5)
    visible = all_pos[None, :] <= query_pos[:, None]
    weights_exp = jnp.where(visible, jnp.exp(scores), 0.0)
    probs = (weights_exp / jnp.sum(weights_exp, axis=-1, keepdims=True)).astype(jnp.bfloat16)
    mixed = (
        jnp.einsum("kgqs,skd->qkgd", probs, value_states, preferred_element_type=jnp.float32)
        .astype(jnp.bfloat16)
        .reshape(query_rows, query_cols)
    )
    attn_partial = jnp.dot(
        lax.all_gather(mixed, "dp", axis=0, tiled=True),
        w_output[0],
        preferred_element_type=jnp.float32,
    )
    attn = lax.psum_scatter(
        attn_partial.astype(jnp.bfloat16), "tensor", scatter_dimension=0, tiled=True
    ).astype(jnp.float32)
    resid = (arrived.astype(jnp.float32) + attn).astype(jnp.bfloat16)
    resid_wide = resid.astype(jnp.float32)
    squares_ffn = lax.psum(jnp.sum(resid_wide * resid_wide, axis=1), "dp")
    normed_ffn = (
        resid_wide * lax.rsqrt(squares_ffn / width_total + EPS)[:, None] * gain_ffn
    ).astype(jnp.bfloat16)
    rows_ffn = lax.all_gather(normed_ffn, "tensor", axis=0, tiled=True)
    ff_dev = w_gate_up.shape[3]
    summed = lax.psum_scatter(
        jnp.einsum("rd,gdf->rgf", rows_ffn, w_gate_up[0], preferred_element_type=jnp.float32)
        .reshape(query_rows * lax.axis_size("dp"), 2 * ff_dev)
        .astype(jnp.bfloat16),
        "dp",
        scatter_dimension=0,
        tiled=True,
    ).astype(jnp.float32)
    hidden = (jax.nn.silu(summed[:, :ff_dev]) * summed[:, ff_dev:]).astype(jnp.bfloat16)
    ffn_partial = jnp.dot(
        lax.all_gather(hidden, "dp", axis=0, tiled=True),
        w_down[0],
        preferred_element_type=jnp.float32,
    )
    ffn = lax.psum_scatter(
        ffn_partial.astype(jnp.bfloat16), "tensor", scatter_dimension=0, tiled=True
    ).astype(jnp.float32)
    result = (resid_wide + ffn).astype(jnp.bfloat16)
    return result[None]


def solution(mesh):
    placed = (
        P("section", "tensor", "dp"),
        P("section", "dp"),
        P("section", "dp", "tensor"),
        P("section", None, "dp", None),
        P("section", "tensor", "dp"),
        P("section", "dp"),
        P("section", None, "dp", "tensor"),
        P("section", "tensor", "dp"),
    )
    return jax.shard_map(
        local, mesh=mesh, in_specs=placed, out_specs=P("section", "tensor", "dp"), check_vma=False
    )
```

profile of v0, /device:TPU:8, one launch (start us, length us, event | category | flops | bytes accessed | tf_op | source)
XLA Modules:
  0.0 766.1 jit_solution(4502816704359785971)
XLA Ops:
  6.5 0.0 copy-start
  6.5 0.0 all-gather.5.cloned.1.call-start
  6.5 7.2 collective-permute-start
  13.7 0.7 mul.231
  14.4 3.1 collective-permute-done
  17.5 0.1 fusion.25
  17.6 38.6 %psum.21 = f32[128]{0:T(128)S(1)} all-reduce(f32[128]{0:T(128)S(1)} %fusion.25), channel_id=1, replica_groups=mesh['section'=2,'dp'=16,'tensor'=8] {'dp'}, use_global_device_ids=true, to_apply=%region_1.2 | all-reduce | flops 128 | bytes 1024 | tf_op jit(solution)/shard_map/psum | solution.py:71
  56.2 0.8 fusion.27
  57.0 0.0 all-gather.5.cloned.1.call-update
  57.0 0.0 all-reduce.2.cloned.1.call-start
  57.1 1.7 dynamic-slice_bitcast_fusion.1
  58.8 27.4 %all-gather.5.cloned.1.call-done = bf16[1024,512]{1,0:T(8,128)(2,1)} async-done(((bf16[128,512]{1,0:T(8,128)(2,1)}), bf16[1024,512]{1,0:T(8,128)(2,1)}) %all-gather.5.cloned.1.call-update) | async-done | bytes 1048592 | tf_op jit(solution)/shard_map/all_gather | solution.py:76
  86.2 2.4 convolution_convert_fusion.1
  88.7 0.8 slice.54
  89.5 0.0 all-reduce.2.cloned.1.call-update
  89.5 0.0 reduce-scatter.5.cloned.1.call-start
  89.6 1.0 slice.59
  90.6 0.0 reduce-scatter.5.cloned.1.call-update
  90.7 0.0 all-gather.7.cloned.1.call-start
  90.8 0.1 iota_compare_fusion
  90.9 0.2 multiply_cosine_fusion.1
  91.1 160.4 %all-reduce.2.cloned.1.call-done = bf16[1024,256]{1,0:T(8,128)(2,1)} async-done(((bf16[1024,256]{1,0:T(8,128)(2,1)}), bf16[1024,256]{1,0:T(8,128)(2,1)}) %all-reduce.2.cloned.1.call-update) | async-done | bytes 524304 | tf_op jit(solution)/shard_map/psum | solution.py:83
  251.5 1.1 fusion.33
  252.6 2.4 fusion.37
  255.0 79.3 %reduce-scatter.5.cloned.1.call-done = bf16[64,512]{1,0:T(8,128)(2,1)} async-done(((bf16[1024,512]{1,0:T(8,128)(2,1)}), bf16[64,512]{1,0:T(8,128)(2,1)}) %reduce-scatter.5.cloned.1.call-update) | async-done | bytes 65552 | tf_op jit(solution)/shard_map/reduce_scatter | solution.py:80
  334.3 0.9 reshape.220
  335.2 0.1 fusion.45
  335.4 0.6 fusion.46
  336.0 0.0 copy-done.2
  336.0 0.4 fusion.8
  336.3 0.0 copy-start.3
  336.4 0.1 copy.13
  336.4 0.6 copy.23
  337.1 0.0 all-gather.7.cloned.1.call-update
  337.1 0.0 reduce-scatter.7.cloned.1.call-start
  337.1 81.5 %all-gather.7.cloned.1.call-done = bf16[1024,512]{1,0:T(8,128)(2,1)} async-done(((bf16[64,512]{1,0:T(8,128)(2,1)}), bf16[1024,512]{1,0:T(8,128)(2,1)}) %all-gather.7.cloned.1.call-update) | async-done | bytes 1048592 | tf_op jit(solution)/shard_map/all_gather | solution.py:104
  418.6 3.0 convolution_convert_fusion.2
  421.7 0.0 reduce-scatter.7.cloned.1.call-update
  421.7 0.0 all-gather.9.cloned.1.call-start
  421.7 0.0 copy-done.3
  421.8 33.3 %reduce-scatter.7.cloned.1.call-done = bf16[128,512]{1,0:T(8,128)(2,1)} async-done(((bf16[1024,512]{1,0:T(8,128)(2,1)}), bf16[128,512]{1,0:T(8,128)(2,1)}) %reduce-scatter.7.cloned.1.call-update) | async-done | bytes 131088 | tf_op jit(solution)/shard_map/reduce_scatter | solution.py:108
  455.1 1.0 fusion.29
  456.1 39.0 %psum.23 = f32[128]{0:T(128)S(1)} all-reduce(f32[128]{0:T(128)S(1)} %fusion.29), channel_id=1, replica_groups=mesh['section'=2,'dp'=16,'tensor'=8] {'dp'}, use_global_device_ids=true, to_apply=%region_7.8 | all-reduce | flops 128 | bytes 1024 | tf_op jit(solution)/shard_map/psum | solution.py:113
  495.1 1.7 fusion.31
  496.7 0.0 all-gather.9.cloned.1.call-update
  496.7 0.0 reduce-scatter.9.cloned.1.call-start
  496.8 6.0 copy.14
  502.8 18.1 %all-gather.9.cloned.1.call-done = bf16[1024,512]{1,0:T(8,128)(2,1)} async-done(((bf16[128,512]{1,0:T(8,128)(2,1)}), bf16[1024,512]{1,0:T(8,128)(2,1)}) %all-gather.9.cloned.1.call-update) | async-done | bytes 1048592 | tf_op jit(solution)/shard_map/all_gather | solution.py:117
  520.9 9.3 %convolution_convert_fusion = bf16[1024,3584]{1,0:T(8,128)(2,1)} fusion(bf16[1024,512]{1,0:T(8,128)(2,1)} %all-gather.9.cloned.1.call-done, bf16[3584,512]{1,0:T(8,128)(2,1)} %bitcast.64), kind=kOutput, calls=%fused_computation | convolution fusion | flops 3761766400 | bytes 12058624 | tf_op jit(solution)/shard_map/rd,gdf->rgf/dot_general | solution.py:120
  530.2 0.0 reduce-scatter.9.cloned.1.call-update
  530.3 0.0 all-gather.11.cloned.1.call-start
  530.3 101.4 %reduce-scatter.9.cloned.1.call-done = bf16[64,3584]{1,0:T(8,128)(2,1)} async-done(((bf16[1024,3584]{1,0:T(8,128)(2,1)}), bf16[64,3584]{1,0:T(8,128)(2,1)}) %reduce-scatter.9.cloned.1.call-update) | async-done | bytes 458768 | tf_op jit(solution)/shard_map/reduce_scatter | solution.py:119
  631.7 1.1 convert_element_type.103
  632.8 0.8 fusion.24
  633.6 0.0 all-gather.11.cloned.1.call-update
  633.6 0.0 copy-start.1
  633.6 0.0 reduce-scatter.11.cloned.1.call-start
  633.7 85.8 %all-gather.11.cloned.1.call-done = bf16[1024,1792]{1,0:T(8,128)(2,1)} async-done(((bf16[64,1792]{1,0:T(8,128)(2,1)}), bf16[1024,1792]{1,0:T(8,128)(2,1)}) %all-gather.11.cloned.1.call-update) | async-done | bytes 3670032 | tf_op jit(solution)/shard_map/all_gather | solution.py:129
  719.4 0.0 copy-done
  719.4 5.1 fusion.2
  724.5 0.0 reduce-scatter.11.cloned.1.call-update
  724.5 33.5 %reduce-scatter.11.cloned.1.call-done = bf16[128,512]{1,0:T(8,128)(2,1)} async-done(((bf16[1024,512]{1,0:T(8,128)(2,1)}), bf16[128,512]{1,0:T(8,128)(2,1)}) %reduce-scatter.11.cloned.1.call-update) | async-done | bytes 131088 | tf_op jit(solution)/shard_map/reduce_scatter | solution.py:133
  758.0 0.0 copy-done.1
  758.0 1.6 fusion.38
  (9 shorter events, 0.1 us)
Async XLA Ops:
  6.5 712.9 %copy-start = (bf16[1,1792,512]{2,1,0:T(8,128)(2,1)S(1)}, bf16[1,1792,512]{2,1,0:T(8,128)(2,1)}, u32[]{:S(2)}) copy-start(bf16[1,1792,512]{2,1,0:T(8,128)(2,1)} %param.15) | copy-start | bytes 5505028
  6.5 79.7 %all-gather.5.cloned.1.call-start = ((), (), s32[]{:S(2)}) async-start(), calls=%async_computation.4 | async-start | bytes 1179648 | tf_op jit(solution)/shard_map/all_gather | solution.py:76
  6.5 11.0 %collective-permute-start = (bf16[128,512]{1,0:T(8,128)(2,1)}, bf16[128,512]{1,0:T(8,128)(2,1)S(1)}, u32[]{:S(2)}, u32[]{:S(2)}) collective-permute-start(bf16[128,512]{1,0:T(8,128)(2,1)} %bitcast.70), channel_id=1, source_target_pairs={{0,128},{128,0},{1,129},{129,1},{2,130},{130,2},{3,131},{131,3},{4... | collective-permute-start | bytes 393224 | tf_op jit(solution)/shard_map/ppermute | solution.py:16
  57.0 194.5 %all-reduce.2.cloned.1.call-start = ((), (), s32[]{:S(2)}) async-start(), calls=%async_computation.5 | async-start | bytes 1048576 | tf_op jit(solution)/shard_map/psum | solution.py:83
  89.5 244.8 %reduce-scatter.5.cloned.1.call-start = ((), (), s32[]{:S(2)}) async-start(), calls=%async_computation.6 | async-start | bytes 1114112 | tf_op jit(solution)/shard_map/reduce_scatter | solution.py:80
  90.7 328.0 %all-gather.7.cloned.1.call-start = ((), (), s32[]{:S(2)}) async-start(), calls=%async_computation.7 | async-start | bytes 1114112 | tf_op jit(solution)/shard_map/all_gather | solution.py:104
  251.5 84.5 %copy-start.2 = (bf16[1024,256]{1,0:T(8,128)(2,1)S(1)}, bf16[1024,256]{1,0:T(8,128)(2,1)}, u32[]{:S(2)}) copy-start(bf16[1024,256]{1,0:T(8,128)(2,1)} %all-reduce.2.cloned.1.call-done) | copy-start | bytes 1572868
  336.3 85.4 %copy-start.3 = (bf16[1,512]{1,0:T(2,128)(2,1)S(1)}, bf16[1,512]{1,0:T(2,128)(2,1)}, u32[]{:S(2)}) copy-start(bf16[1,512]{1,0:T(2,128)(2,1)} %param.13) | copy-start | bytes 3076
  337.1 118.0 %reduce-scatter.7.cloned.1.call-start = ((), (), s32[]{:S(2)}) async-start(), calls=%async_computation.8 | async-start | bytes 1179648 | tf_op jit(solution)/shard_map/reduce_scatter | solution.py:108
  421.7 99.2 %all-gather.9.cloned.1.call-start = ((), (), s32[]{:S(2)}) async-start(), calls=%async_computation.9 | async-start | bytes 1179648 | tf_op jit(solution)/shard_map/all_gather | solution.py:117
  496.7 134.9 %reduce-scatter.9.cloned.1.call-start = ((), (), s32[]{:S(2)}) async-start(), calls=%async_computation.10 | async-start | bytes 7798784 | tf_op jit(solution)/shard_map/reduce_scatter | solution.py:119
  530.3 189.1 %all-gather.11.cloned.1.call-start = ((), (), s32[]{:S(2)}) async-start(), calls=%async_computation.11 | async-start | bytes 3899392 | tf_op jit(solution)/shard_map/all_gather | solution.py:129
  633.6 124.4 %copy-start.1 = (bf16[128,512]{1,0:T(8,128)(2,1)S(1)}, bf16[128,512]{1,0:T(8,128)(2,1)}, u32[]{:S(2)}) copy-start(bf16[128,512]{1,0:T(8,128)(2,1)} %reduce-scatter.7.cloned.1.call-done) | copy-start | bytes 393220
  633.6 124.4 %reduce-scatter.11.cloned.1.call-start = ((), (), s32[]{:S(2)}) async-start(), calls=%async_computation.12 | async-start | bytes 1179648 | tf_op jit(solution)/shard_map/reduce_scatter | solution.py:133
Sparse Core Ops, SparseCore 0:
  57.2 29.0 all-gather.4
  89.7 161.8 all-reduce.1
  254.0 80.2 reduce-scatter.4
  337.2 81.3 all-gather.6
  421.8 33.1 reduce-scatter.6
  496.9 24.0 all-gather.8
  530.4 101.2 reduce-scatter.8
  633.7 85.6 all-gather.10
  724.7 33.2 reduce-scatter.10
where the time goes:
time: 767 us; the launch traced here: 766 us
  waiting for transfers between devices  624 us (81%)
  blocking collectives  77.6 us (10%)
  matrix products  20.8 us (3%)
  between operations  13.4 us (2%)
  other arithmetic  11.6 us (2%)
  local copies, waits for them, and re-layouts  11.3 us (1%)
    psum x1, waiting for transfers between devices, local(): lax.psum(partial_qkv[:, query_cols:].astype(jnp.bfloat16), 'dp')  160 us
    reduce_scatter x1, waiting for transfers between devices, local(): lax.psum_scatter(jnp.einsum('rd,gdf->rgf', rows_ffn, w_gate_up[0], prefer...  101 us
    all_gather x1, waiting for transfers between devices, local(): lax.all_gather(hidden, 'dp', axis=0, tiled=True)  85.8 us
    all_gather x1, waiting for transfers between devices, local(): lax.all_gather(mixed, 'dp', axis=0, tiled=True)  81.5 us
    reduce_scatter x1, waiting for transfers between devices, local(): lax.psum_scatter(partial_qkv[:, :query_cols].astype(jnp.bfloat16), 'dp',...  79.3 us
    psum x1, blocking collectives, local(): squares_ffn = lax.psum(jnp.sum(resid_wide * resid_wide, axis=1), 'dp')  39 us
    psum x1, blocking collectives, local(): squares = lax.psum(jnp.sum(wide * wide, axis=1), 'dp')  38.6 us
    reduce_scatter x1, waiting for transfers between devices, local(): lax.psum_scatter(ffn_partial.astype(jnp.bfloat16), 'tensor', scatter_dime...  33.5 us
  transfers between devices with their start and end apart: 10, of which 10 were waited for; matrix products, arithmetic and copies ran while one was open for 2% of the time, Pallas kernels for 0%

commit v1 on v0

--- a/solution.py
+++ b/solution.py
@@ -9,6 +9,14 @@
 KEY_VALUE_HEADS = 4
 EPS = 1e-05
 THETA = 500000.0
+
+
+def fit_frame_on_mesh(q_in):
+    e_now = lax.axis_size("dp")
+    side_arr = jnp.stack([q_in] * e_now, axis=0)
+    arr_next = lax.all_to_all(side_arr, split_axis=0, concat_axis=0, axis_name="dp")
+    o_now = jnp.concatenate(arr_next, axis=0)
+    return o_now
 
 
 def from_behind(x, axis, by):
@@ -101,9 +109,7 @@
         .reshape(query_rows, query_cols)
     )
     attn_partial = jnp.dot(
-        lax.all_gather(mixed, "dp", axis=0, tiled=True),
-        w_output[0],
-        preferred_element_type=jnp.float32,
+        fit_frame_on_mesh(mixed), w_output[0], preferred_element_type=jnp.float32
     )
     attn = lax.psum_scatter(
         attn_partial.astype(jnp.bfloat16), "tensor", scatter_dimension=0, tiled=True

time: 767 us -> 708 us (0.923)
  waiting for transfers between devices: 624 us -> 544 us
  blocking collectives: 77.6 us -> 101 us
    all_gather x1 -> x0, waiting for transfers between devices: 81.5 us -> none  [local(): lax.all_gather(mixed, 'dp', axis=0, tiled=True)]
    all_to_all x0 -> x1, blocking collectives: none -> 23.4 us  [fit_frame_on_mesh(): lax.all_to_all(side_arr, split_axis=0, concat_axis=0, axis_name='dp')]
  transfers between devices with their start and end apart: 10 -> 9, of which waited for: 10 -> 9; matrix products, arithmetic and copies ran while one was open for 2% -> 2% of each run, Pallas kernels for 0% -> 0%
where the time goes in v1:
time: 708 us
  waiting for transfers between devices  544 us (77%)
  blocking collectives  101 us (14%)
  matrix products  19.4 us (3%)
  between operations  13.7 us (2%)
  other arithmetic  11.6 us (2%)
  local copies, waits for them, and re-layouts  10.8 us (2%)
  starting transfers between devices  7.48 us (1%)
    psum x1, waiting for transfers between devices, local(): lax.psum(partial_qkv[:, query_cols:].astype(jnp.bfloat16), 'dp')  160 us
    reduce_scatter x1, waiting for transfers between devices, local(): lax.psum_scatter(jnp.einsum('rd,gdf->rgf', rows_ffn, w_gate_up[0], prefer...  101 us
    all_gather x1, waiting for transfers between devices, local(): lax.all_gather(hidden, 'dp', axis=0, tiled=True)  86.1 us
    reduce_scatter x1, waiting for transfers between devices, local(): lax.psum_scatter(partial_qkv[:, :query_cols].astype(jnp.bfloat16), 'dp',...  79.3 us
    psum x1, blocking collectives, local(): squares_ffn = lax.psum(jnp.sum(resid_wide * resid_wide, axis=1), 'dp')  38.9 us
    psum x1, blocking collectives, local(): squares = lax.psum(jnp.sum(wide * wide, axis=1), 'dp')  38.6 us
    reduce_scatter x1, waiting for transfers between devices, local(): lax.psum_scatter(attn_partial.astype(jnp.bfloat16), 'tensor', scatter_dim...  34.6 us
    reduce_scatter x1, waiting for transfers between devices, local(): lax.psum_scatter(ffn_partial.astype(jnp.bfloat16), 'tensor', scatter_dime...  33.5 us
  transfers between devices with their start and end apart: 9, of which 9 were waited for; matrix products, arithmetic and copies ran while one was open for 2% of the time, Pallas kernels for 0%

profile of v1, /device:TPU:8, one launch (start us, length us, event | category | flops | bytes accessed | tf_op | source)
XLA Modules:
  0.0 707.5 jit_solution(14938330568051807353)
XLA Ops:
  6.5 0.0 copy-start
  6.5 0.0 all-gather.4.cloned.1.call-start
  6.5 7.2 %collective-permute-start = (bf16[128,512]{1,0:T(8,128)(2,1)}, bf16[128,512]{1,0:T(8,128)(2,1)S(1)}, u32[]{:S(2)}, u32[]{:S(2)}) collective-permute-start(bf16[128,512]{1,0:T(8,128)(2,1)} %bitcast.72), channel_id=1, source_target_pairs={{0,128},{128,0},{1,129},{129,1},{2,130},{130,2},{3,131},{131,3},{4... | collective-permute-start | bytes 393224 | tf_op jit(solution)/shard_map/ppermute | solution.py:24
  13.7 0.7 mul.231
  14.4 3.1 collective-permute-done
  17.5 0.1 fusion.25
  17.6 38.6 %psum.21 = f32[128]{0:T(128)S(1)} all-reduce(f32[128]{0:T(128)S(1)} %fusion.25), channel_id=1, replica_groups=mesh['section'=2,'dp'=16,'tensor'=8] {'dp'}, use_global_device_ids=true, to_apply=%region_1.2 | all-reduce | flops 128 | bytes 1024 | tf_op jit(solution)/shard_map/psum | solution.py:79
  56.2 0.8 fusion.27
  57.0 0.0 all-gather.4.cloned.1.call-update
  57.0 0.0 all-reduce.2.cloned.1.call-start
  57.1 1.7 dynamic-slice_bitcast_fusion.1
  58.8 27.4 %all-gather.4.cloned.1.call-done = bf16[1024,512]{1,0:T(8,128)(2,1)} async-done(((bf16[128,512]{1,0:T(8,128)(2,1)}), bf16[1024,512]{1,0:T(8,128)(2,1)}) %all-gather.4.cloned.1.call-update) | async-done | bytes 1048592 | tf_op jit(solution)/shard_map/all_gather | solution.py:84
  86.2 2.4 convolution_convert_fusion.1
  88.7 0.8 slice.54
  89.5 0.0 all-reduce.2.cloned.1.call-update
  89.5 0.0 reduce-scatter.5.cloned.1.call-start
  89.6 1.1 slice.59
  90.6 0.0 reduce-scatter.5.cloned.1.call-update
  90.7 0.0 reduce-scatter.7.cloned.1.call-start
  90.8 0.1 iota_compare_fusion
  90.9 0.2 multiply_cosine_fusion.1
  91.1 160.4 %all-reduce.2.cloned.1.call-done = bf16[1024,256]{1,0:T(8,128)(2,1)} async-done(((bf16[1024,256]{1,0:T(8,128)(2,1)}), bf16[1024,256]{1,0:T(8,128)(2,1)}) %all-reduce.2.cloned.1.call-update) | async-done | bytes 524304 | tf_op jit(solution)/shard_map/psum | solution.py:91
  251.5 1.1 fusion.33
  252.6 2.4 fusion.37
  255.0 79.3 %reduce-scatter.5.cloned.1.call-done = bf16[64,512]{1,0:T(8,128)(2,1)} async-done(((bf16[1024,512]{1,0:T(8,128)(2,1)}), bf16[64,512]{1,0:T(8,128)(2,1)}) %reduce-scatter.5.cloned.1.call-update) | async-done | bytes 65552 | tf_op jit(solution)/shard_map/reduce_scatter | solution.py:88
  334.4 0.9 reshape.222
  335.2 0.1 fusion.45
  335.4 0.6 fusion.46
  336.0 0.0 copy-done.2
  336.0 0.0 copy-start.4
  336.0 0.4 fusion.8
  336.4 0.1 copy.13
  336.4 0.1 stack.3
  336.5 0.0 copy-start.3
  336.6 23.4 %all_to_all.5 = bf16[16,64,512]{2,1,0:T(8,128)(2,1)S(1)} all-to-all(bf16[16,64,512]{2,1,0:T(8,128)(2,1)S(1)} %stack.3), channel_id=1, replica_groups=mesh['section'=2,'dp'=16,'tensor'=8] {'dp'}, dimensions={0} | all-to-all | bytes 2097152 | tf_op jit(solution)/shard_map/all_to_all | solution.py:17
  360.0 0.0 copy-done.4
  360.0 1.7 convolution_convert_fusion.2
  361.7 0.0 reduce-scatter.7.cloned.1.call-update
  361.7 0.0 all-gather.6.cloned.1.call-start
  361.7 0.0 copy-done.3
  361.8 34.6 %reduce-scatter.7.cloned.1.call-done = bf16[128,512]{1,0:T(8,128)(2,1)} async-done(((bf16[1024,512]{1,0:T(8,128)(2,1)}), bf16[128,512]{1,0:T(8,128)(2,1)}) %reduce-scatter.7.cloned.1.call-update) | async-done | bytes 131088 | tf_op jit(solution)/shard_map/reduce_scatter | solution.py:114
  396.3 1.0 fusion.29
  397.4 38.9 %psum.23 = f32[128]{0:T(128)S(1)} all-reduce(f32[128]{0:T(128)S(1)} %fusion.29), channel_id=1, replica_groups=mesh['section'=2,'dp'=16,'tensor'=8] {'dp'}, use_global_device_ids=true, to_apply=%region_7.8 | all-reduce | flops 128 | bytes 1024 | tf_op jit(solution)/shard_map/psum | solution.py:119
  436.3 1.7 fusion.31
  438.0 0.0 all-gather.6.cloned.1.call-update
  438.0 0.0 reduce-scatter.9.cloned.1.call-start
  438.0 6.0 copy.14
  444.0 18.2 %all-gather.6.cloned.1.call-done = bf16[1024,512]{1,0:T(8,128)(2,1)} async-done(((bf16[128,512]{1,0:T(8,128)(2,1)}), bf16[1024,512]{1,0:T(8,128)(2,1)}) %all-gather.6.cloned.1.call-update) | async-done | bytes 1048592 | tf_op jit(solution)/shard_map/all_gather | solution.py:123
  462.2 9.3 %convolution_convert_fusion = bf16[1024,3584]{1,0:T(8,128)(2,1)} fusion(bf16[1024,512]{1,0:T(8,128)(2,1)} %all-gather.6.cloned.1.call-done, bf16[3584,512]{1,0:T(8,128)(2,1)} %bitcast.65), kind=kOutput, calls=%fused_computation | convolution fusion | flops 3761766400 | bytes 12058624 | tf_op jit(solution)/shard_map/rd,gdf->rgf/dot_general | solution.py:126
  471.5 0.0 reduce-scatter.9.cloned.1.call-update
  471.5 0.0 all-gather.8.cloned.1.call-start
  471.6 100.8 %reduce-scatter.9.cloned.1.call-done = bf16[64,3584]{1,0:T(8,128)(2,1)} async-done(((bf16[1024,3584]{1,0:T(8,128)(2,1)}), bf16[64,3584]{1,0:T(8,128)(2,1)}) %reduce-scatter.9.cloned.1.call-update) | async-done | bytes 458768 | tf_op jit(solution)/shard_map/reduce_scatter | solution.py:125
  572.4 1.1 convert_element_type.103
  573.5 0.8 fusion.24
  574.3 0.0 all-gather.8.cloned.1.call-update
  574.3 0.0 copy-start.1
  574.3 0.0 reduce-scatter.11.cloned.1.call-start
  574.4 86.1 %all-gather.8.cloned.1.call-done = bf16[1024,1792]{1,0:T(8,128)(2,1)} async-done(((bf16[64,1792]{1,0:T(8,128)(2,1)}), bf16[1024,1792]{1,0:T(8,128)(2,1)}) %all-gather.8.cloned.1.call-update) | async-done | bytes 3670032 | tf_op jit(solution)/shard_map/all_gather | solution.py:135
  660.5 0.0 copy-done
  660.5 5.1 fusion.2
  665.6 0.0 reduce-scatter.11.cloned.1.call-update
  665.6 33.5 %reduce-scatter.11.cloned.1.call-done = bf16[128,512]{1,0:T(8,128)(2,1)} async-done(((bf16[1024,512]{1,0:T(8,128)(2,1)}), bf16[128,512]{1,0:T(8,128)(2,1)}) %reduce-scatter.11.cloned.1.call-update) | async-done | bytes 131088 | tf_op jit(solution)/shard_map/reduce_scatter | solution.py:139
  699.1 0.0 copy-done.1
  699.1 1.6 fusion.38
  (10 shorter events, 0.1 us)
Async XLA Ops:
  6.5 654.0 %copy-start = (bf16[1,1792,512]{2,1,0:T(8,128)(2,1)S(1)}, bf16[1,1792,512]{2,1,0:T(8,128)(2,1)}, u32[]{:S(2)}) copy-start(bf16[1,1792,512]{2,1,0:T(8,128)(2,1)} %param.15) | copy-start | bytes 5505028
  6.5 79.7 %all-gather.4.cloned.1.call-start = ((), (), s32[]{:S(2)}) async-start(), calls=%async_computation.5 | async-start | bytes 1179648 | tf_op jit(solution)/shard_map/all_gather | solution.py:84
  6.5 11.0 %collective-permute-start = (bf16[128,512]{1,0:T(8,128)(2,1)}, bf16[128,512]{1,0:T(8,128)(2,1)S(1)}, u32[]{:S(2)}, u32[]{:S(2)}) collective-permute-start(bf16[128,512]{1,0:T(8,128)(2,1)} %bitcast.72), channel_id=1, source_target_pairs={{0,128},{128,0},{1,129},{129,1},{2,130},{130,2},{3,131},{131,3},{4... | collective-permute-start | bytes 393224 | tf_op jit(solution)/shard_map/ppermute | solution.py:24
  57.0 194.5 %all-reduce.2.cloned.1.call-start = ((), (), s32[]{:S(2)}) async-start(), calls=%async_computation.6 | async-start | bytes 1048576 | tf_op jit(solution)/shard_map/psum | solution.py:91
  89.5 244.8 %reduce-scatter.5.cloned.1.call-start = ((), (), s32[]{:S(2)}) async-start(), calls=%async_computation.7 | async-start | bytes 1114112 | tf_op jit(solution)/shard_map/reduce_scatter | solution.py:88
  90.7 305.7 %reduce-scatter.7.cloned.1.call-start = ((), (), s32[]{:S(2)}) async-start(), calls=%async_computation.8 | async-start | bytes 1179648 | tf_op jit(solution)/shard_map/reduce_scatter | solution.py:114
  251.5 84.5 %copy-start.2 = (bf16[1024,256]{1,0:T(8,128)(2,1)S(1)}, bf16[1024,256]{1,0:T(8,128)(2,1)}, u32[]{:S(2)}) copy-start(bf16[1024,256]{1,0:T(8,128)(2,1)} %all-reduce.2.cloned.1.call-done) | copy-start | bytes 1572868
  336.0 24.0 %copy-start.4 = (bf16[1,512,512]{2,1,0:T(8,128)(2,1)S(1)}, bf16[1,512,512]{2,1,0:T(8,128)(2,1)}, u32[]{:S(2)}) copy-start(bf16[1,512,512]{2,1,0:T(8,128)(2,1)} %param.12) | copy-start | bytes 1572868
  336.5 25.2 %copy-start.3 = (bf16[1,512]{1,0:T(2,128)(2,1)S(1)}, bf16[1,512]{1,0:T(2,128)(2,1)}, u32[]{:S(2)}) copy-start(bf16[1,512]{1,0:T(2,128)(2,1)} %param.13) | copy-start | bytes 3076
  361.7 100.5 %all-gather.6.cloned.1.call-start = ((), (), s32[]{:S(2)}) async-start(), calls=%async_computation.9 | async-start | bytes 1179648 | tf_op jit(solution)/shard_map/all_gather | solution.py:123
  438.0 134.4 %reduce-scatter.9.cloned.1.call-start = ((), (), s32[]{:S(2)}) async-start(), calls=%async_computation.10 | async-start | bytes 7798784 | tf_op jit(solution)/shard_map/reduce_scatter | solution.py:125
  471.5 189.0 %all-gather.8.cloned.1.call-start = ((), (), s32[]{:S(2)}) async-start(), calls=%async_computation.11 | async-start | bytes 3899392 | tf_op jit(solution)/shard_map/all_gather | solution.py:135
  574.3 124.8 %copy-start.1 = (bf16[128,512]{1,0:T(8,128)(2,1)S(1)}, bf16[128,512]{1,0:T(8,128)(2,1)}, u32[]{:S(2)}) copy-start(bf16[128,512]{1,0:T(8,128)(2,1)} %reduce-scatter.7.cloned.1.call-done) | copy-start | bytes 393220
  574.3 124.7 %reduce-scatter.11.cloned.1.call-start = ((), (), s32[]{:S(2)}) async-start(), calls=%async_computation.12 | async-start | bytes 1179648 | tf_op jit(solution)/shard_map/reduce_scatter | solution.py:139
Sparse Core Ops, SparseCore 0:
  57.2 29.0 all-gather.3
  89.7 161.8 all-reduce.1
  254.0 80.2 reduce-scatter.4
  361.8 34.4 reduce-scatter.6
  438.1 24.0 all-gather.5
  471.7 100.7 reduce-scatter.8
  574.5 86.0 all-gather.7
  665.8 33.2 reduce-scatter.10
